TPU v7x, 32 devices: a whole 2x2x4 slice. The times are simulated.
32 devices in a mesh: rows: 8 (over z, y), ch: 4 (over x, core).
Axes of the slice: x: 2, y: 2, z: 4, core: 2. Of those that a mesh axis runs over, the one named last changes fastest.
Arguments:
- tile_image: bfloat16 [768, 256, 256], P('ch', 'rows'), may hold values from -23 to 23
- spectral_filter: float32 [2, 768, 256, 256], P(None, 'ch', 'rows'), may hold values from -4 to 4
- conv_taps: float32 [768, 9], P('ch'), may hold values from -4 to 4
- norm_gain: float32 [768], replicated, may hold values from 0.25 to 1.75
- up_weight: bfloat16 [768, 3072], P(None, 'ch'), may hold values from -0.21875 to 0.21875
- down_weight: bfloat16 [3072, 768], P('ch'), may hold values from -0.109375 to 0.109375
- upstream: bfloat16 [768, 256, 256], P('ch', 'rows'), may hold values from -5 to 5
Outputs:
- block_out: bfloat16 [768, 256, 256], P('ch', 'rows')
- grad_image: float32 [768, 256, 256], P('ch', 'rows')
- grad_filter: float32 [2, 768, 256, 256], P(None, 'ch', 'rows')
All inputs are finite; a program needn't handle non-finite values.
Results may differ from a plain program's by a relative error of at most 0.012.
Values may be sent and summed in bfloat16 or wider, within the bound.
A program may use at most 192 MiB of HBM per device.

v0:
```python
import math

import jax
import jax.numpy as jnp
from jax import lax
from jax.sharding import PartitionSpec as P

norm_epsilon = 1e-05
root_half = 0.7071067811865476
density = 0.3989422804014327


def with_halo(block, sides, width):
    for axis, dim in sides:
        count = lax.axis_size(axis)
        forward = [(i, i + 1) for i in range(count - 1)]
        backward = [(target, source) for source, target in forward]
        low = lax.ppermute(
            lax.slice_in_dim(block, block.shape[dim] - width, None, axis=dim), axis, forward
        )
        high = lax.ppermute(lax.slice_in_dim(block, 0, width, axis=dim), axis, backward)
        block = jnp.concatenate([low, block, high], axis=dim)
    return block


def contract(form, left, right):
    return jnp.einsum(
        form, left, right, precision=lax.Precision.HIGHEST, preferred_element_type=jnp.float32
    )


def angle_tables(length):
    indices = jnp.arange(length, dtype=jnp.int32)
    products = indices[:, None] * indices[None, :] % length
    angles = products.astype(jnp.float32) * (2.0 * math.pi / length)
    return (jnp.cos(angles), jnp.sin(angles))


def filter_pass(signal, kernel_re, kernel_im):
    col_len = signal.shape[2]
    cos_w, sin_w = angle_tables(col_len)
    head_re = contract("chw,kw->ckh", signal, cos_w)
    head_im = -contract("chw,kw->ckh", signal, sin_w)
    col_re, col_im = (
        lax.all_to_all(
            head_re.astype(jnp.bfloat16), "rows", split_axis=1, concat_axis=2, tiled=True
        ).astype(head_re.dtype),
        lax.all_to_all(
            head_im.astype(jnp.bfloat16), "rows", split_axis=1, concat_axis=2, tiled=True
        ).astype(head_im.dtype),
    )
    row_len = col_re.shape[2]
    cos_h, sin_h = angle_tables(row_len)
    spec_re = contract("cwh,kh->cwk", col_re, cos_h) + contract("cwh,kh->cwk", col_im, sin_h)
    spec_im = contract("cwh,kh->cwk", col_im, cos_h) - contract("cwh,kh->cwk", col_re, sin_h)
    prod_re = kernel_re * spec_re - kernel_im * spec_im
    prod_im = kernel_re * spec_im + kernel_im * spec_re
    back_re = contract("cwk,kh->cwh", prod_re, cos_h) - contract("cwk,kh->cwh", prod_im, sin_h)
    back_im = contract("cwk,kh->cwh", prod_im, cos_h) + contract("cwk,kh->cwh", prod_re, sin_h)
    row_re, row_im = (
        lax.all_to_all(
            back_re.astype(jnp.bfloat16), "rows", split_axis=2, concat_axis=1, tiled=True
        ).astype(back_re.dtype),
        lax.all_to_all(
            back_im.astype(jnp.bfloat16), "rows", split_axis=2, concat_axis=1, tiled=True
        ).astype(back_im.dtype),
    )
    outcome = contract("ckh,kw->chw", row_re, cos_w) - contract("ckh,kw->chw", row_im, sin_w)
    return (outcome * (1.0 / (row_len * col_len)), spec_re, spec_im)


def depthwise(signal, tap_weights):
    token_row_count, col_count = (signal.shape[1], signal.shape[2])
    padded = with_halo(signal.astype(jnp.bfloat16), (("rows", 1),), 1).astype(signal.dtype)
    padded = jnp.pad(padded, ((0, 0), (0, 0), (1, 1)))
    running = jnp.zeros_like(signal)
    for row_off in range(3):
        for col_off in range(3):
            running = (
                running
                + tap_weights[:, 3 * row_off + col_off][:, None, None]
                * padded[:, row_off : row_off + token_row_count, col_off : col_off + col_count]
            )
    return running


def layer_norm(whole):
    values = whole.astype(jnp.float32)
    centred = values - jnp.mean(values, axis=0)[None]
    inv_std = lax.rsqrt(jnp.mean(centred * centred, axis=0) + norm_epsilon)
    return (centred * inv_std[None], inv_std)


def gelu_slope(pre_act):
    return 0.5 * (1.0 + lax.erf(pre_act * root_half)) + pre_act * density * jnp.exp(
        -0.5 * pre_act * pre_act
    )


def norm_back(normed_gradient, normed, inv_std, gain):
    weighted = normed_gradient * gain[None, :, None, None]
    mean_one = jnp.mean(weighted, axis=1, keepdims=True)
    second = jnp.mean(weighted * normed[None], axis=1, keepdims=True)
    return inv_std[None, None] * (weighted - mean_one - normed[None] * second)


def settle(partials):
    return jnp.sum(
        lax.optimization_barrier(partials.astype(jnp.bfloat16)).astype(jnp.float32), axis=0
    )


def to_tokens(values):
    return lax.all_to_all(values, "ch", split_axis=2, concat_axis=0, tiled=True)


def to_channels(values):
    return lax.all_to_all(
        values.astype(jnp.bfloat16), "ch", split_axis=0, concat_axis=2, tiled=True
    ).astype(values.dtype)


def on_device(tile_image, spectral_filter, conv_taps, norm_gain, up_weight, down_weight, upstream):
    signal = tile_image.astype(jnp.float32)
    filtered, spec_re, spec_im = filter_pass(signal, spectral_filter[0], spectral_filter[1])
    hidden_state = signal + depthwise(filtered, conv_taps)
    rounded = hidden_state.astype(jnp.bfloat16)
    gain_column = norm_gain[:, None, None]
    full_up, full_down = (
        lax.all_gather(up_weight, "ch", axis=1, tiled=True),
        lax.all_gather(down_weight, "ch", axis=0, tiled=True),
    )
    blocks = lax.axis_size("ch")
    channels, hidden_units = (full_up.shape[0], full_up.shape[1])
    hidden_share_units = hidden_units // blocks
    normed, inv_std = layer_norm(to_tokens(rounded))
    scaled = (normed * gain_column).astype(jnp.bfloat16)
    pre_act = jnp.einsum("chw,cf->fhw", scaled, full_up, preferred_element_type=jnp.float32)
    activated = jax.nn.gelu(pre_act, approximate=False).astype(jnp.bfloat16)
    token_row_count, col_count = (activated.shape[1], activated.shape[2])
    partials = jnp.einsum(
        "bfhw,bfc->bchw",
        activated.reshape(blocks, hidden_share_units, token_row_count, col_count),
        full_down.reshape(blocks, hidden_share_units, channels),
        preferred_element_type=jnp.float32,
    )
    out_sum = to_channels(settle(partials))
    block_out = (hidden_state + out_sum).astype(jnp.bfloat16)
    whole_dy = to_tokens(upstream)
    grad_act = jnp.einsum("chw,fc->fhw", whole_dy, full_down, preferred_element_type=jnp.float32)
    preactivation_gradient = (grad_act * gelu_slope(pre_act)).astype(jnp.bfloat16)
    normed_gradient = jnp.einsum(
        "pjra,spj->psra",
        preactivation_gradient.reshape(blocks, hidden_share_units, token_row_count, col_count),
        full_up.reshape(channels, blocks, hidden_share_units),
        preferred_element_type=jnp.float32,
    )
    grad_mlp = to_channels(settle(norm_back(normed_gradient, normed, inv_std, norm_gain)))
    grad_hidden = upstream.astype(jnp.float32) + grad_mlp
    grad_filtered = depthwise(grad_hidden, conv_taps[:, ::-1])
    adjoint, grad_re, grad_im = filter_pass(grad_filtered, spectral_filter[0], -spectral_filter[1])
    grad_image = grad_hidden + adjoint
    factor = 1.0 / (tile_image.shape[2] * spec_re.shape[2])
    grad_filter = jnp.stack(
        [
            (grad_re * spec_re + grad_im * spec_im) * factor,
            (grad_im * spec_re - grad_re * spec_im) * factor,
        ]
    )
    return (block_out, grad_image, grad_filter)


def solution(mesh):
    return jax.shard_map(
        on_device,
        mesh=mesh,
        in_specs=(
            P("ch", "rows", None),
            P(None, "ch", "rows", None),
            P("ch", None),
            P(),
            P(None, "ch"),
            P("ch", None),
            P("ch", "rows", None),
        ),
        out_specs=(P("ch", "rows", None), P("ch", "rows", None), P(None, "ch", "rows", None)),
        check_vma=False,
    )
```

profile of v0, /device:TPU:0, one launch (start us, length us, event | category | flops | bytes accessed | tf_op | source)
XLA Modules:
  0.0 1455.8 jit_solution(15047290855060164912)
XLA Ops:
  48.5 77.4 %all-to-all-done.1 = bf16[192,256,32]{0,2,1:T(8,128)(2,1)} async-done(((bf16[192,256,32]{0,2,1:T(8,128)(2,1)}), bf16[192,256,32]{0,2,1:T(8,128)(2,1)}, u32[]{:S(2)}, u32[]{:S(2)}) %all-to-all-start.1) | async-done | bytes 3145760 | tf_op jit(solution)/shard_map/all_to_all | solution.py:48
  148.2 75.1 %all-to-all-done = bf16[192,256,32]{0,2,1:T(8,128)(2,1)} async-done(((bf16[192,256,32]{0,2,1:T(8,128)(2,1)}), bf16[192,256,32]{0,2,1:T(8,128)(2,1)}, u32[]{:S(2)}, u32[]{:S(2)}) %all-to-all-start) | async-done | bytes 3145760 | tf_op jit(solution)/shard_map/all_to_all | solution.py:45
  250.0 15.3 %fusion.64 = (f32[192,32,256]{2,1,0:T(8,128)}, f32[192,32,256]{2,1,0:T(8,128)}, f32[192,32,256]{2,1,0:T(8,128)}) fusion(f32[192,32,256]{2,1,0:T(8,128)} %convolution_subtract_fusion.1, f32[2,192,32,256]{3,2,1,0:T(8,128)} %param.8, f32[192,32,256]{2,1,0:T(8,128)} %fusion.125, bf16[192,32,256]{2,1,0:T(8,128)(2,1)S(1)} %copy.223), kind=kOutput, calls=%fused_computation.102 | convolution fusion | flops 4843765760 | bytes 47185920 | tf_op jit(solution)/shard_map/cwh,kh->cwk/dot_general | solution.py:27
  323.1 64.0 %all-to-all-done.2 = bf16[192,32,256]{0,1,2:T(8,128)(2,1)} async-done(((bf16[192,32,256]{0,1,2:T(8,128)(2,1)}), bf16[192,32,256]{0,1,2:T(8,128)(2,1)}, u32[]{:S(2)}, u32[]{:S(2)}) %all-to-all-start.2) | async-done | bytes 3145760 | tf_op jit(solution)/shard_map/all_to_all | solution.py:61
  413.2 71.0 %all-to-all-done.3 = bf16[192,32,256]{0,1,2:T(8,128)(2,1)} async-done(((bf16[192,32,256]{0,1,2:T(8,128)(2,1)}), bf16[192,32,256]{0,1,2:T(8,128)(2,1)}, u32[]{:S(2)}, u32[]{:S(2)}) %all-to-all-start.3) | async-done | bytes 3145760 | tf_op jit(solution)/shard_map/all_to_all | solution.py:64
  530.0 37.9 %fusion.253 = (bf16[192,32,256]{2,1,0:T(8,128)(2,1)S(1)}, f32[192,32,256]{2,1,0:T(8,128)}) fusion(f32[192]{0:T(256)S(1)} %bitcast.308, f32[192,34,256]{2,1,0:T(8,128)} %maximum_convert_fusion, f32[192]{0:T(256)S(1)} %bitcast.310, f32[192]{0:T(256)S(1)} %bitcast.296, f32[192]{0:T(256)S(1)} %bitcast.298, f32[192]{0:T(256)S(1)} %bitcast.300, ...), kind=kLoop, calls=%fused_computation.292 | loop fusion | flops 31457280 | bytes 39328512 | tf_op jit(solution)/shard_map/convert_element_type | solution.py:127
  603.4 16.1 %fusion.261 = f32[3072,2048]{0,1} fusion(bf16[3072,768]{1,0:T(8,128)(2,1)} %all-gather.5.cloned.1.call-done, bf16[768,2048]{0,1:T(8,128)(2,1)S(1)} %reshape.95), kind=kOutput, calls=%fused_computation.297 | convolution fusion | flops 9663676416 | bytes 33030144
  637.0 13.8 copy.236
  669.4 80.0 %fusion.7 = (bf16[3072,32,64]{0,2,1:T(8,128)(2,1)}, bf16[3072,32,64]{0,2,1:T(8,128)(2,1)}) fusion(f32[3072,32,64]{0,2,1:T(8,128)} %bitcast.313, bf16[768,3072]{1,0:T(8,128)(2,1)S(1)} %bitcast.292, f32[768,32,64]{0,2,1:T(8,128)S(1)} %subtract_multiply_fusion, f32[768]{0:T(1024)S(1)} %copy-done.33), kind=kOutput, calls=%fused_computation.9 | convolution fusion | flops 10138681344 | bytes 61344768 | tf_op jit(solution)/shard_map/chw,cf->fhw/dot_general | solution.py:138
  749.4 22.7 %bitcast_reduce_fusion = (f32[4,32,64]{2,1,0:T(8,128)S(1)}, f32[4,32,64]{2,1,0:T(8,128)S(1)}, f32[4,32,64,768]{3,2,1,0:T(8,128)}) fusion(f32[768]{0:T(1024)S(1)} %copy-done.33, f32[768,32,64]{0,2,1:T(8,128)} %copy-done.9, bf16[768,4,768,1]{2,1,0,3:T(4,128)(2,1)} %bitcast.293, bf16[32,8,4,8,768]{4,3,2,1,0:T(8,128)(2,1)} %bitcast.315), kind=kOutput, calls=%fused_computation.12 | convolution fusion | flops 9688825856 | bytes 48827392 | tf_op jit(solution)/shard_map/pjra,spj->psra/dot_general | solution.py:152
  772.1 16.0 %fusion.10 = bf16[4,768,32,64]{1,3,2,0:T(8,128)(2,1)} fusion(f32[4,32,64,768]{3,2,1,0:T(8,128)} %get-tuple-element.33, f32[4,32,64]{2,1,0:T(8,128)S(1)} %get-tuple-element.34, f32[768,32,64]{0,2,1:T(8,128)} %copy-done.9, f32[4,32,64]{2,1,0:T(8,128)S(1)} %get-tuple-element.35, f32[768]{0:T(1024)S(1)} %copy-done.33, f32[32,64]{1,0:T(8,128)S(1)} %copy-done.13), kind=kLoop, calls=%fused_computation.15 | loop fusion | flops 37748736 | bytes 44116992 | tf_op jit(solution)/shard_map/convert_element_type | solution.py:109
  811.6 40.3 %all_to_all.189 = bf16[4,2,196608]{2,1,0:T(2,128)(2,1)} all-to-all(bf16[4,2,196608]{2,1,0:T(2,128)(2,1)S(1)} %reshape.101), channel_id=1, replica_groups=mesh['rows'=8,'ch'=4] {'ch'}, dimensions={0} | all-to-all | bytes 6291456 | tf_op jit(solution)/shard_map/all_to_all | solution.py:118
  912.3 15.1 %fusion.57 = f32[192,32,256]{2,1,0:T(8,128)} fusion(f32[192,34,256]{2,1,0:T(8,128)S(1)} %maximum_convert_fusion.1, f32[192]{0:T(256)S(1)} %bitcast.309, f32[192]{0:T(256)S(1)} %bitcast.311, f32[192]{0:T(256)S(1)} %bitcast.297, f32[192]{0:T(256)S(1)} %bitcast.299, f32[192]{0:T(256)S(1)} %bitcast.301, f32[192]{0:T(256)S(1)} %bitcast.303, f32[192]{0:T(256)S(1)} %bitcast.305, ...), kind=kLoop, calls=%fused_computation.86 | loop fusion | flops 26738688 | bytes 33039360 | tf_op jit(solution)/shard_map/add | solution.py:80
  927.4 12.5 fusion.77
  950.4 12.5 convert_bitcast_fusion.2
  968.7 75.3 %all-to-all-done.9 = bf16[192,256,32]{0,2,1:T(8,128)(2,1)} async-done(((bf16[192,256,32]{0,2,1:T(8,128)(2,1)}), bf16[192,256,32]{0,2,1:T(8,128)(2,1)}, u32[]{:S(2)}, u32[]{:S(2)}) %all-to-all-start.9) | async-done | bytes 3145760 | tf_op jit(solution)/shard_map/all_to_all | solution.py:48
  1048.8 17.0 %convert_bitcast_fusion = bf16[4,768,32,64]{1,3,2,0:T(8,128)(2,1)} fusion(bf16[4,768,768,1]{2,1,3,0:T(8,128)(2,1)} %bitcast.312, bf16[32,8,4,8,768]{4,3,2,1,0:T(8,128)(2,1)} %bitcast.314), kind=kOutput, calls=%fused_computation.60 | convolution fusion | flops 9669967872 | bytes 29884416 | tf_op jit(solution)/shard_map/bfhw,bfc->bchw/dot_general | solution.py:141
  1107.7 33.9 %all-to-all-done.8 = bf16[192,256,32]{0,2,1:T(8,128)(2,1)} async-done(((bf16[192,256,32]{0,2,1:T(8,128)(2,1)}), bf16[192,256,32]{0,2,1:T(8,128)(2,1)}, u32[]{:S(2)}, u32[]{:S(2)}) %all-to-all-start.8) | async-done | bytes 3145760 | tf_op jit(solution)/shard_map/all_to_all | solution.py:45
  1176.4 23.1 %multiply_bitcast_fusion.1 = (f32[1,192,32,256]{3,2,1,0:T(8,128)}, f32[1,192,32,256]{3,2,1,0:T(8,128)}, f32[192,32,256]{2,1,0:T(8,128)}, f32[192,32,256]{2,1,0:T(8,128)}) fusion(f32[192,32,256]{2,1,0:T(8,128)} %convolution_subtract_fusion, f32[192,32,256]{2,1,0:T(8,128)S(1)} %bitcast.270, f32[192,32,256]{2,1,0:T(8,128)} %get-tuple-element.32, ...), kind=kOutput, calls=%fused_computation.110 | convolution fusion | flops 4857921536 | bytes 66060288 | tf_op jit(solution)/shard_map/cwh,kh->cwk/dot_general | solution.py:27
  1199.5 11.1 fusion.110
  1229.3 10.9 fusion.106
  1257.0 66.3 %all-to-all-done.10 = bf16[192,32,256]{0,1,2:T(8,128)(2,1)} async-done(((bf16[192,32,256]{0,1,2:T(8,128)(2,1)}), bf16[192,32,256]{0,1,2:T(8,128)(2,1)}, u32[]{:S(2)}, u32[]{:S(2)}) %all-to-all-start.10) | async-done | bytes 3145760 | tf_op jit(solution)/shard_map/all_to_all | solution.py:61
  1406.4 15.1 %all-to-all-done.11 = bf16[192,32,256]{0,1,2:T(8,128)(2,1)} async-done(((bf16[192,32,256]{0,1,2:T(8,128)(2,1)}), bf16[192,32,256]{0,1,2:T(8,128)(2,1)}, u32[]{:S(2)}, u32[]{:S(2)}) %all-to-all-start.11) | async-done | bytes 3145760 | tf_op jit(solution)/shard_map/all_to_all | solution.py:64
  1436.7 12.0 multiply_add_fusion
  (199 shorter events, 606.0 us)
Async XLA Ops:
  24.9 101.0 %all-to-all-start.1 = ((bf16[192,256,32]{0,2,1:T(8,128)(2,1)}), bf16[192,256,32]{0,2,1:T(8,128)(2,1)}, u32[]{:S(2)}, u32[]{:S(2)}) async-start(bf16[192,256,32]{0,2,1:T(8,128)(2,1)} %copy.221), calls=%async_computation.1 | async-start | bytes 8388608 | tf_op jit(solution)/shard_map/all_to_all | solution.py:48
  126.0 97.3 %all-to-all-start = ((bf16[192,256,32]{0,2,1:T(8,128)(2,1)}), bf16[192,256,32]{0,2,1:T(8,128)(2,1)}, u32[]{:S(2)}, u32[]{:S(2)}) async-start(bf16[192,256,32]{0,2,1:T(8,128)(2,1)} %copy.217), calls=%async_computation | async-start | bytes 8388608 | tf_op jit(solution)/shard_map/all_to_all | solution.py:45
  290.0 97.1 %all-to-all-start.2 = ((bf16[192,32,256]{0,1,2:T(8,128)(2,1)}), bf16[192,32,256]{0,1,2:T(8,128)(2,1)}, u32[]{:S(2)}, u32[]{:S(2)}) async-start(bf16[192,32,256]{0,1,2:T(8,128)(2,1)} %copy.226), calls=%async_computation.2 | async-start | bytes 8388608 | tf_op jit(solution)/shard_map/all_to_all | solution.py:61
  294.6 299.0 %all-gather.3.cloned.1.call-start = ((), (), s32[]{:S(2)}) async-start(), calls=%async_computation.12 | async-start | bytes 5898240 | tf_op jit(solution)/shard_map/all_gather | solution.py:130
  323.1 69.4 %copy-start.3 = (bf16[192,32,256]{2,1,0:T(8,128)(2,1)S(1)}, bf16[192,32,256]{2,1,0:T(8,128)(2,1)}, u32[]{:S(2)}) copy-start(bf16[192,32,256]{2,1,0:T(8,128)(2,1)} %param.13) | copy-start | bytes 9437188
  387.2 97.1 %all-to-all-start.3 = ((bf16[192,32,256]{0,1,2:T(8,128)(2,1)}), bf16[192,32,256]{0,1,2:T(8,128)(2,1)}, u32[]{:S(2)}, u32[]{:S(2)}) async-start(bf16[192,32,256]{0,1,2:T(8,128)(2,1)} %copy.230), calls=%async_computation.3 | async-start | bytes 8388608 | tf_op jit(solution)/shard_map/all_to_all | solution.py:64
  391.8 211.7 %all-gather.5.cloned.1.call-start = ((), (), s32[]{:S(2)}) async-start(), calls=%async_computation.13 | async-start | bytes 5898240 | tf_op jit(solution)/shard_map/all_gather | solution.py:131
  484.3 90.1 %all-to-all-start.6 = ((bf16[192,32,256]{0,1,2:T(8,128)(2,1)}), bf16[192,32,256]{0,1,2:T(8,128)(2,1)}, u32[]{:S(2)}, u32[]{:S(2)}) async-start(bf16[192,32,256]{0,1,2:T(8,128)(2,1)} %copy.242), calls=%async_computation.6 | async-start | bytes 8388608 | tf_op jit(solution)/shard_map/all_to_all | solution.py:114
  512.4 9.2 collective-permute-start.1
  513.7 12.0 collective-permute-start
  518.5 49.4 %copy-start.14 = (f32[192,1]{0,1:T(1,128)}, f32[192,1]{0,1:T(1,128)S(1)}, u32[]{:S(2)}) copy-start(f32[192,1]{0,1:T(1,128)S(1)} %get-tuple-element.23) | copy-start | bytes 2308
  518.5 49.4 %copy-start.16 = (f32[192,1]{0,1:T(1,128)}, f32[192,1]{0,1:T(1,128)S(1)}, u32[]{:S(2)}) copy-start(f32[192,1]{0,1:T(1,128)S(1)} %get-tuple-element.24) | copy-start | bytes 2308
  518.5 49.4 %copy-start.18 = (f32[192,1]{0,1:T(1,128)}, f32[192,1]{0,1:T(1,128)S(1)}, u32[]{:S(2)}) copy-start(f32[192,1]{0,1:T(1,128)S(1)} %get-tuple-element.25) | copy-start | bytes 2308
  518.5 49.4 %copy-start.20 = (f32[192,1]{0,1:T(1,128)}, f32[192,1]{0,1:T(1,128)S(1)}, u32[]{:S(2)}) copy-start(f32[192,1]{0,1:T(1,128)S(1)} %get-tuple-element.26) | copy-start | bytes 2308
  518.6 49.4 %copy-start.22 = (f32[192,1]{0,1:T(1,128)}, f32[192,1]{0,1:T(1,128)S(1)}, u32[]{:S(2)}) copy-start(f32[192,1]{0,1:T(1,128)S(1)} %get-tuple-element.27) | copy-start | bytes 2308
  574.3 53.1 %all-to-all-start.4 = ((bf16[192,32,256]{0,1,2:T(8,128)(2,1)}), bf16[192,32,256]{0,1,2:T(8,128)(2,1)}, u32[]{:S(2)}, u32[]{:S(2)}) async-start(bf16[192,32,256]{0,1,2:T(8,128)(2,1)} %copy.234), calls=%async_computation.4 | async-start | bytes 8388608 | tf_op jit(solution)/shard_map/all_to_all | solution.py:114
  669.4 80.0 %copy-start.9 = (f32[768,32,64]{0,2,1:T(8,128)}, f32[768,32,64]{0,2,1:T(8,128)S(1)}, u32[]{:S(2)}) copy-start(f32[768,32,64]{0,2,1:T(8,128)S(1)} %subtract_multiply_fusion) | copy-start | bytes 18874372
  896.2 8.9 collective-permute-start.3
  897.5 12.0 collective-permute-start.2
  945.6 98.4 %all-to-all-start.9 = ((bf16[192,256,32]{0,2,1:T(8,128)(2,1)}), bf16[192,256,32]{0,2,1:T(8,128)(2,1)}, u32[]{:S(2)}, u32[]{:S(2)}) async-start(bf16[192,256,32]{0,2,1:T(8,128)(2,1)} %copy.256), calls=%async_computation.9 | async-start | bytes 8388608 | tf_op jit(solution)/shard_map/all_to_all | solution.py:48
  1044.0 97.6 %all-to-all-start.8 = ((bf16[192,256,32]{0,2,1:T(8,128)(2,1)}), bf16[192,256,32]{0,2,1:T(8,128)(2,1)}, u32[]{:S(2)}, u32[]{:S(2)}) async-start(bf16[192,256,32]{0,2,1:T(8,128)(2,1)} %copy.252), calls=%async_computation.8 | async-start | bytes 8388608 | tf_op jit(solution)/shard_map/all_to_all | solution.py:45
  1141.6 82.8 %all-to-all-start.5 = ((bf16[4,2,196608]{2,1,0:T(2,128)(2,1)}), bf16[4,2,196608]{2,1,0:T(2,128)(2,1)}, u32[]{:S(2)}, u32[]{:S(2)}) async-start(bf16[4,2,196608]{2,1,0:T(2,128)(2,1)} %reshape.99), calls=%async_computation.5 | async-start | bytes 6291456 | tf_op jit(solution)/shard_map/all_to_all | solution.py:118
  1224.4 99.0 %all-to-all-start.10 = ((bf16[192,32,256]{0,1,2:T(8,128)(2,1)}), bf16[192,32,256]{0,1,2:T(8,128)(2,1)}, u32[]{:S(2)}, u32[]{:S(2)}) async-start(bf16[192,32,256]{0,1,2:T(8,128)(2,1)} %copy.261), calls=%async_computation.10 | async-start | bytes 8388608 | tf_op jit(solution)/shard_map/all_to_all | solution.py:61
  1323.3 98.2 %all-to-all-start.11 = ((bf16[192,32,256]{0,1,2:T(8,128)(2,1)}), bf16[192,32,256]{0,1,2:T(8,128)(2,1)}, u32[]{:S(2)}, u32[]{:S(2)}) async-start(bf16[192,32,256]{0,1,2:T(8,128)(2,1)} %copy.265), calls=%async_computation.11 | async-start | bytes 8388608 | tf_op jit(solution)/shard_map/all_to_all | solution.py:64
  (37 other events, 588.5 us)
Sparse Core Ops, SparseCore 0:
  297.0 38.7 all-gather.2
  394.1 38.7 all-gather.4
where the time goes:
time: 1470 us; the launch traced here: 1460 us
  waiting for transfers between devices  501 us (34%)
  matrix products  365 us (25%)
  local copies, waits for them, and re-layouts  336 us (23%)
  other arithmetic  129 us (9%)
  starting transfers between devices  69 us (5%)
  blocking collectives  40.3 us (3%)
  between operations  15.2 us (1%)
    dot_general x24, matrix products, contract(): jnp.einsum(form, left, right, precision=lax.Precision.HIGHEST, preferred_...  229 us
    all_to_all x2, waiting for transfers between devices, filter_pass(): lax.all_to_all(head_im.astype(jnp.bfloat16), 'rows', split_axis=1, concat...  153 us
    all_to_all x2, waiting for transfers between devices, filter_pass(): lax.all_to_all(back_re.astype(jnp.bfloat16), 'rows', split_axis=2, concat...  130 us
    all_to_all x2, waiting for transfers between devices, filter_pass(): lax.all_to_all(head_re.astype(jnp.bfloat16), 'rows', split_axis=1, concat...  109 us
    all_to_all x2, waiting for transfers between devices, filter_pass(): lax.all_to_all(back_im.astype(jnp.bfloat16), 'rows', split_axis=2, concat...  86.2 us
    dot_general x1, matrix products, on_device(): jnp.einsum('chw,cf->fhw', scaled, full_up, preferred_element_type=jnp.flo...  80 us
    convert_element_type x6, local copies, waits for them, and re-layouts, to_channels(): return lax.all_to_all(values.astype(jnp.bfloat16), 'ch', split_axis=0, co...  50.7 us
    unnamed x94, local copies, waits for them, and re-layouts  43.1 us
  transfers between devices with their start and end apart: 17, of which 13 were waited for; matrix products, arithmetic and copies ran while one was open for 31% of the time, Pallas kernels for 0%

commit v1 on v0

--- a/solution.py
+++ b/solution.py
@@ -25,7 +25,10 @@
 
 def contract(form, left, right):
     return jnp.einsum(
-        form, left, right, precision=lax.Precision.HIGHEST, preferred_element_type=jnp.float32
+        form,
+        left.astype(jnp.bfloat16),
+        right.astype(jnp.bfloat16),
+        preferred_element_type=jnp.float32,
     )
 
 

time: 1470 us -> 1420 us (0.966)
  matrix products: 365 us -> 271 us
  waiting for transfers between devices: 501 us -> 543 us
    dot_general x24, matrix products: 229 us -> 135 us  [contract(): jnp.einsum(form, left.astype(jnp.bfloat16), right.astype(jnp.bfloat16), p...]
    all_to_all x2, waiting for transfers between devices: 130 us -> 160 us  [filter_pass(): lax.all_to_all(back_re.astype(jnp.bfloat16), 'rows', split_axis=2, concat...]
    convert_element_type x0 -> x1, other arithmetic: none -> 15.2 us  [contract(): left.astype(jnp.bfloat16)]
    add x1 -> x0, other arithmetic: 15.1 us -> none  [depthwise(): running + tap_weights[:, 3 * row_off + col_off][:, None, None] * padded[:...]
    unnamed x94 -> x92, local copies, waits for them, and re-layouts: 43.1 us -> 44.9 us
  transfers between devices with their start and end apart: 17 -> 17, of which waited for: 13 -> 13; matrix products, arithmetic and copies ran while one was open for 31% -> 28% of each run, Pallas kernels for 0% -> 0%
where the time goes in v1:
time: 1420 us; the launch traced here: 1410 us
  waiting for transfers between devices  543 us (38%)
  local copies, waits for them, and re-layouts  342 us (24%)
  matrix products  271 us (19%)
  other arithmetic  130 us (9%)
  starting transfers between devices  66.9 us (5%)
  blocking collectives  40.2 us (3%)
  between operations  15.4 us (1%)
    all_to_all x2, waiting for transfers between devices, filter_pass(): lax.all_to_all(back_re.astype(jnp.bfloat16), 'rows', split_axis=2, concat...  160 us
    all_to_all x2, waiting for transfers between devices, filter_pass(): lax.all_to_all(head_im.astype(jnp.bfloat16), 'rows', split_axis=1, concat...  159 us
    dot_general x24, matrix products, contract(): jnp.einsum(form, left.astype(jnp.bfloat16), right.astype(jnp.bfloat16), p...  135 us
    all_to_all x2, waiting for transfers between devices, filter_pass(): lax.all_to_all(head_re.astype(jnp.bfloat16), 'rows', split_axis=1, concat...  113 us
    all_to_all x2, waiting for transfers between devices, filter_pass(): lax.all_to_all(back_im.astype(jnp.bfloat16), 'rows', split_axis=2, concat...  87.9 us
    dot_general x1, matrix products, on_device(): jnp.einsum('chw,cf->fhw', scaled, full_up, preferred_element_type=jnp.flo...  80 us
    convert_element_type x6, local copies, waits for them, and re-layouts, to_channels(): return lax.all_to_all(values.astype(jnp.bfloat16), 'ch', split_axis=0, co...  50.7 us
    unnamed x92, local copies, waits for them, and re-layouts  44.9 us
  transfers between devices with their start and end apart: 17, of which 13 were waited for; matrix products, arithmetic and copies ran while one was open for 28% of the time, Pallas kernels for 0%

profile of v1, /device:TPU:0, one launch (start us, length us, event | category | flops | bytes accessed | tf_op | source)
XLA Modules:
  0.0 1407.7 jit_solution(16746754535843758968)
XLA Ops:
  44.2 79.5 %all-to-all-done.1 = bf16[192,256,32]{0,2,1:T(8,128)(2,1)} async-done(((bf16[192,256,32]{0,2,1:T(8,128)(2,1)}), bf16[192,256,32]{0,2,1:T(8,128)(2,1)}, u32[]{:S(2)}, u32[]{:S(2)}) %all-to-all-start.1) | async-done | bytes 3145760 | tf_op jit(solution)/shard_map/all_to_all | solution.py:51
  144.1 77.0 %all-to-all-done = bf16[192,256,32]{0,2,1:T(8,128)(2,1)} async-done(((bf16[192,256,32]{0,2,1:T(8,128)(2,1)}), bf16[192,256,32]{0,2,1:T(8,128)(2,1)}, u32[]{:S(2)}, u32[]{:S(2)}) %all-to-all-start) | async-done | bytes 3145760 | tf_op jit(solution)/shard_map/all_to_all | solution.py:48
  241.6 13.1 fusion.67
  287.7 75.8 %all-to-all-done.2 = bf16[192,32,256]{0,1,2:T(8,128)(2,1)} async-done(((bf16[192,32,256]{0,1,2:T(8,128)(2,1)}), bf16[192,32,256]{0,1,2:T(8,128)(2,1)}, u32[]{:S(2)}, u32[]{:S(2)}) %all-to-all-start.2) | async-done | bytes 3145760 | tf_op jit(solution)/shard_map/all_to_all | solution.py:64
  389.7 70.9 %all-to-all-done.3 = bf16[192,32,256]{0,1,2:T(8,128)(2,1)} async-done(((bf16[192,32,256]{0,1,2:T(8,128)(2,1)}), bf16[192,32,256]{0,1,2:T(8,128)(2,1)}, u32[]{:S(2)}, u32[]{:S(2)}) %all-to-all-start.3) | async-done | bytes 3145760 | tf_op jit(solution)/shard_map/all_to_all | solution.py:67
  502.6 37.9 %fusion.234 = (bf16[192,32,256]{2,1,0:T(8,128)(2,1)S(1)}, f32[192,32,256]{2,1,0:T(8,128)}) fusion(f32[192]{0:T(256)S(1)} %bitcast.288, f32[192,34,256]{2,1,0:T(8,128)} %maximum_convert_fusion, f32[192]{0:T(256)S(1)} %bitcast.290, f32[192]{0:T(256)S(1)} %bitcast.276, f32[192]{0:T(256)S(1)} %bitcast.278, f32[192]{0:T(256)S(1)} %bitcast.280, ...), kind=kLoop, calls=%fused_computation.275 | loop fusion | flops 31457280 | bytes 39328512 | tf_op jit(solution)/shard_map/convert_element_type | solution.py:130
  566.2 9.7 reshape.83
  576.0 15.8 %fusion.242 = f32[3072,2048]{0,1} fusion(bf16[3072,768]{1,0:T(8,128)(2,1)} %all-gather.5.cloned.1.call-done, bf16[768,2048]{0,1:T(8,128)(2,1)S(1)} %reshape.95), kind=kOutput, calls=%fused_computation.280 | convolution fusion | flops 9663676416 | bytes 33030144
  600.0 9.6 fusion.236
  609.6 13.8 copy.236
  623.4 10.2 reshape.84
  642.0 80.0 %fusion.7 = (bf16[3072,32,64]{0,2,1:T(8,128)(2,1)}, bf16[3072,32,64]{0,2,1:T(8,128)(2,1)}) fusion(f32[3072,32,64]{0,2,1:T(8,128)} %bitcast.293, bf16[768,3072]{1,0:T(8,128)(2,1)S(1)} %bitcast.272, f32[768,32,64]{0,2,1:T(8,128)S(1)} %subtract_multiply_fusion, f32[768]{0:T(1024)S(1)} %copy-done.38), kind=kOutput, calls=%fused_computation.9 | convolution fusion | flops 10138681344 | bytes 61344768 | tf_op jit(solution)/shard_map/chw,cf->fhw/dot_general | solution.py:141
  721.9 22.7 %bitcast_reduce_fusion = (f32[4,32,64]{2,1,0:T(8,128)S(1)}, f32[4,32,64]{2,1,0:T(8,128)S(1)}, f32[4,32,64,768]{3,2,1,0:T(8,128)}) fusion(f32[768]{0:T(1024)S(1)} %copy-done.38, f32[768,32,64]{0,2,1:T(8,128)} %copy-done.13, bf16[768,4,768,1]{2,1,0,3:T(4,128)(2,1)} %bitcast.273, bf16[32,8,4,8,768]{4,3,2,1,0:T(8,128)(2,1)} %bitcast.295), kind=kOutput, calls=%fused_computation.12 | convolution fusion | flops 9688825856 | bytes 48827392 | tf_op jit(solution)/shard_map/pjra,spj->psra/dot_general | solution.py:155
  744.7 16.0 %fusion.10 = bf16[4,768,32,64]{1,3,2,0:T(8,128)(2,1)} fusion(f32[4,32,64,768]{3,2,1,0:T(8,128)} %get-tuple-element.33, f32[4,32,64]{2,1,0:T(8,128)S(1)} %get-tuple-element.34, f32[768,32,64]{0,2,1:T(8,128)} %copy-done.13, f32[4,32,64]{2,1,0:T(8,128)S(1)} %get-tuple-element.35, f32[768]{0:T(1024)S(1)} %copy-done.38, f32[32,64]{1,0:T(8,128)S(1)} %copy-done.18), kind=kLoop, calls=%fused_computation.15 | loop fusion | flops 37748736 | bytes 44116992 | tf_op jit(solution)/shard_map/convert_element_type | solution.py:112
  768.0 9.8 copy.247
  784.3 40.2 %all_to_all.189 = bf16[4,2,196608]{2,1,0:T(2,128)(2,1)} all-to-all(bf16[4,2,196608]{2,1,0:T(2,128)(2,1)S(1)} %reshape.101), channel_id=1, replica_groups=mesh['rows'=8,'ch'=4] {'ch'}, dimensions={0} | all-to-all | bytes 6291456 | tf_op jit(solution)/shard_map/all_to_all | solution.py:121
  884.7 15.2 %fusion.58 = bf16[192,32,256]{2,1,0:T(8,128)(2,1)} fusion(f32[192,34,256]{2,1,0:T(8,128)S(1)} %maximum_convert_fusion.1, f32[192]{0:T(256)S(1)} %bitcast.289, f32[192]{0:T(256)S(1)} %bitcast.291, f32[192]{0:T(256)S(1)} %bitcast.277, f32[192]{0:T(256)S(1)} %bitcast.279, f32[192]{0:T(256)S(1)} %bitcast.281, f32[192]{0:T(256)S(1)} %bitcast.283, ...), kind=kLoop, calls=%fused_computation.87 | loop fusion | flops 28311552 | bytes 29893632 | tf_op jit(solution)/shard_map/convert_element_type | solution.py:29
  934.5 79.7 %all-to-all-done.9 = bf16[192,256,32]{0,2,1:T(8,128)(2,1)} async-done(((bf16[192,256,32]{0,2,1:T(8,128)(2,1)}), bf16[192,256,32]{0,2,1:T(8,128)(2,1)}, u32[]{:S(2)}, u32[]{:S(2)}) %all-to-all-start.9) | async-done | bytes 3145760 | tf_op jit(solution)/shard_map/all_to_all | solution.py:51
  1019.2 17.0 %convert_bitcast_fusion = bf16[4,768,32,64]{1,3,2,0:T(8,128)(2,1)} fusion(bf16[4,768,768,1]{2,1,3,0:T(8,128)(2,1)} %bitcast.292, bf16[32,8,4,8,768]{4,3,2,1,0:T(8,128)(2,1)} %bitcast.294), kind=kOutput, calls=%fused_computation.60 | convolution fusion | flops 9669967872 | bytes 29884416 | tf_op jit(solution)/shard_map/bfhw,bfc->bchw/dot_general | solution.py:144
  1076.2 35.8 %all-to-all-done.8 = bf16[192,256,32]{0,2,1:T(8,128)(2,1)} async-done(((bf16[192,256,32]{0,2,1:T(8,128)(2,1)}), bf16[192,256,32]{0,2,1:T(8,128)(2,1)}, u32[]{:S(2)}, u32[]{:S(2)}) %all-to-all-start.8) | async-done | bytes 3145760 | tf_op jit(solution)/shard_map/all_to_all | solution.py:48
  1142.9 21.4 %multiply_bitcast_fusion.1 = (f32[1,192,32,256]{3,2,1,0:T(8,128)}, f32[1,192,32,256]{3,2,1,0:T(8,128)}, bf16[192,32,256]{2,1,0:T(8,128)(2,1)}, bf16[192,32,256]{2,1,0:T(8,128)(2,1)}) fusion(f32[192,32,256]{2,1,0:T(8,128)} %convolution_subtract_fusion, f32[192,32,256]{2,1,0:T(8,128)} %copy-done, f32[192,32,256]{2,1,0:T(8,128)} %get-tuple-element.32, ...), kind=kOutput, calls=%fused_computation.115 | convolution fusion | flops 834600960 | bytes 59768832 | tf_op jit(solution)/shard_map/cwh,kh->cwk/dot_general | solution.py:27
  1194.8 83.9 %all-to-all-done.10 = bf16[192,32,256]{0,1,2:T(8,128)(2,1)} async-done(((bf16[192,32,256]{0,1,2:T(8,128)(2,1)}), bf16[192,32,256]{0,1,2:T(8,128)(2,1)}, u32[]{:S(2)}, u32[]{:S(2)}) %all-to-all-start.10) | async-done | bytes 3145760 | tf_op jit(solution)/shard_map/all_to_all | solution.py:64
  1330.7 9.7 pad_maximum_fusion
  1359.5 17.0 %all-to-all-done.11 = bf16[192,32,256]{0,1,2:T(8,128)(2,1)} async-done(((bf16[192,32,256]{0,1,2:T(8,128)(2,1)}), bf16[192,32,256]{0,1,2:T(8,128)(2,1)}, u32[]{:S(2)}, u32[]{:S(2)}) %all-to-all-start.11) | async-done | bytes 3145760 | tf_op jit(solution)/shard_map/all_to_all | solution.py:67
  (194 shorter events, 530.7 us)
Async XLA Ops:
  23.1 100.6 %all-to-all-start.1 = ((bf16[192,256,32]{0,2,1:T(8,128)(2,1)}), bf16[192,256,32]{0,2,1:T(8,128)(2,1)}, u32[]{:S(2)}, u32[]{:S(2)}) async-start(bf16[192,256,32]{0,2,1:T(8,128)(2,1)} %copy.221), calls=%async_computation.1 | async-start | bytes 8388608 | tf_op jit(solution)/shard_map/all_to_all | solution.py:51
  123.7 97.3 %all-to-all-start = ((bf16[192,256,32]{0,2,1:T(8,128)(2,1)}), bf16[192,256,32]{0,2,1:T(8,128)(2,1)}, u32[]{:S(2)}, u32[]{:S(2)}) async-start(bf16[192,256,32]{0,2,1:T(8,128)(2,1)} %copy.217), calls=%async_computation | async-start | bytes 8388608 | tf_op jit(solution)/shard_map/all_to_all | solution.py:48
  266.3 97.1 %all-to-all-start.2 = ((bf16[192,32,256]{0,1,2:T(8,128)(2,1)}), bf16[192,32,256]{0,1,2:T(8,128)(2,1)}, u32[]{:S(2)}, u32[]{:S(2)}) async-start(bf16[192,32,256]{0,1,2:T(8,128)(2,1)} %copy.226), calls=%async_computation.2 | async-start | bytes 8388608 | tf_op jit(solution)/shard_map/all_to_all | solution.py:64
  270.9 295.3 %all-gather.3.cloned.1.call-start = ((), (), s32[]{:S(2)}) async-start(), calls=%async_computation.12 | async-start | bytes 5898240 | tf_op jit(solution)/shard_map/all_gather | solution.py:133
  287.7 81.1 %copy-start.2 = (bf16[192,32,256]{2,1,0:T(8,128)(2,1)S(1)}, bf16[192,32,256]{2,1,0:T(8,128)(2,1)}, u32[]{:S(2)}) copy-start(bf16[192,32,256]{2,1,0:T(8,128)(2,1)} %param.13) | copy-start | bytes 9437188
  363.4 97.1 %all-to-all-start.3 = ((bf16[192,32,256]{0,1,2:T(8,128)(2,1)}), bf16[192,32,256]{0,1,2:T(8,128)(2,1)}, u32[]{:S(2)}, u32[]{:S(2)}) async-start(bf16[192,32,256]{0,1,2:T(8,128)(2,1)} %copy.230), calls=%async_computation.3 | async-start | bytes 8388608 | tf_op jit(solution)/shard_map/all_to_all | solution.py:67
  368.0 207.9 %all-gather.5.cloned.1.call-start = ((), (), s32[]{:S(2)}) async-start(), calls=%async_computation.13 | async-start | bytes 5898240 | tf_op jit(solution)/shard_map/all_gather | solution.py:134
  460.6 86.3 %all-to-all-start.6 = ((bf16[192,32,256]{0,1,2:T(8,128)(2,1)}), bf16[192,32,256]{0,1,2:T(8,128)(2,1)}, u32[]{:S(2)}, u32[]{:S(2)}) async-start(bf16[192,32,256]{0,1,2:T(8,128)(2,1)} %copy.242), calls=%async_computation.6 | async-start | bytes 8388608 | tf_op jit(solution)/shard_map/all_to_all | solution.py:117
  484.6 9.2 collective-permute-start.1
  485.9 11.9 collective-permute-start
  490.5 50.0 %copy-start.19 = (f32[192,1]{0,1:T(1,128)}, f32[192,1]{0,1:T(1,128)S(1)}, u32[]{:S(2)}) copy-start(f32[192,1]{0,1:T(1,128)S(1)} %get-tuple-element.23) | copy-start | bytes 2308
  490.5 50.0 %copy-start.21 = (f32[192,1]{0,1:T(1,128)}, f32[192,1]{0,1:T(1,128)S(1)}, u32[]{:S(2)}) copy-start(f32[192,1]{0,1:T(1,128)S(1)} %get-tuple-element.24) | copy-start | bytes 2308
  490.5 50.0 %copy-start.23 = (f32[192,1]{0,1:T(1,128)}, f32[192,1]{0,1:T(1,128)S(1)}, u32[]{:S(2)}) copy-start(f32[192,1]{0,1:T(1,128)S(1)} %get-tuple-element.25) | copy-start | bytes 2308
  490.5 50.0 %copy-start.25 = (f32[192,1]{0,1:T(1,128)}, f32[192,1]{0,1:T(1,128)S(1)}, u32[]{:S(2)}) copy-start(f32[192,1]{0,1:T(1,128)S(1)} %get-tuple-element.26) | copy-start | bytes 2308
  490.5 50.0 %copy-start.27 = (f32[192,1]{0,1:T(1,128)}, f32[192,1]{0,1:T(1,128)S(1)}, u32[]{:S(2)}) copy-start(f32[192,1]{0,1:T(1,128)S(1)} %get-tuple-element.27) | copy-start | bytes 2308
  546.9 53.1 %all-to-all-start.4 = ((bf16[192,32,256]{0,1,2:T(8,128)(2,1)}), bf16[192,32,256]{0,1,2:T(8,128)(2,1)}, u32[]{:S(2)}, u32[]{:S(2)}) async-start(bf16[192,32,256]{0,1,2:T(8,128)(2,1)} %copy.234), calls=%async_computation.4 | async-start | bytes 8388608 | tf_op jit(solution)/shard_map/all_to_all | solution.py:117
  641.9 80.0 %copy-start.13 = (f32[768,32,64]{0,2,1:T(8,128)}, f32[768,32,64]{0,2,1:T(8,128)S(1)}, u32[]{:S(2)}) copy-start(f32[768,32,64]{0,2,1:T(8,128)S(1)} %subtract_multiply_fusion) | copy-start | bytes 18874372
  868.8 8.9 collective-permute-start.3
  870.1 12.0 collective-permute-start.2
  916.0 98.2 %all-to-all-start.9 = ((bf16[192,256,32]{0,2,1:T(8,128)(2,1)}), bf16[192,256,32]{0,2,1:T(8,128)(2,1)}, u32[]{:S(2)}, u32[]{:S(2)}) async-start(bf16[192,256,32]{0,2,1:T(8,128)(2,1)} %copy.256), calls=%async_computation.9 | async-start | bytes 8388608 | tf_op jit(solution)/shard_map/all_to_all | solution.py:51
  1014.2 97.7 %all-to-all-start.8 = ((bf16[192,256,32]{0,2,1:T(8,128)(2,1)}), bf16[192,256,32]{0,2,1:T(8,128)(2,1)}, u32[]{:S(2)}, u32[]{:S(2)}) async-start(bf16[192,256,32]{0,2,1:T(8,128)(2,1)} %copy.252), calls=%async_computation.8 | async-start | bytes 8388608 | tf_op jit(solution)/shard_map/all_to_all | solution.py:48
  1111.9 68.0 %all-to-all-start.5 = ((bf16[4,2,196608]{2,1,0:T(2,128)(2,1)}), bf16[4,2,196608]{2,1,0:T(2,128)(2,1)}, u32[]{:S(2)}, u32[]{:S(2)}) async-start(bf16[4,2,196608]{2,1,0:T(2,128)(2,1)} %reshape.99), calls=%async_computation.5 | async-start | bytes 6291456 | tf_op jit(solution)/shard_map/all_to_all | solution.py:121
  1179.9 98.8 %all-to-all-start.10 = ((bf16[192,32,256]{0,1,2:T(8,128)(2,1)}), bf16[192,32,256]{0,1,2:T(8,128)(2,1)}, u32[]{:S(2)}, u32[]{:S(2)}) async-start(bf16[192,32,256]{0,1,2:T(8,128)(2,1)} %copy.261), calls=%async_computation.10 | async-start | bytes 8388608 | tf_op jit(solution)/shard_map/all_to_all | solution.py:64
  1278.7 97.8 %all-to-all-start.11 = ((bf16[192,32,256]{0,1,2:T(8,128)(2,1)}), bf16[192,32,256]{0,1,2:T(8,128)(2,1)}, u32[]{:S(2)}, u32[]{:S(2)}) async-start(bf16[192,32,256]{0,1,2:T(8,128)(2,1)} %copy.265), calls=%async_computation.11 | async-start | bytes 8388608 | tf_op jit(solution)/shard_map/all_to_all | solution.py:67
  (36 other events, 522.7 us)
Sparse Core Ops, SparseCore 0:
  273.3 38.7 all-gather.2
  370.4 38.7 all-gather.4
